TPU v7x, 32 devices: a whole 2x2x4 slice. The times are simulated.
32 devices in a mesh: dp: 8 (over z, x), bn: 4 (over y, core).
Axes of the slice: x: 2, y: 2, z: 4, core: 2. Of those that a mesh axis runs over, the one named last changes fastest.
Arguments:
- features: bfloat16 [128, 19, 19, 1024], P(('dp', 'bn')), may hold values from -8 to 8
- image_counts: int32 [32], P(('dp', 'bn')), may hold values from 2 to 4, as said below
- map_sides: int32 [128], P(('dp', 'bn')), may hold values from 13 to 19, as said below
- split_kernel: bfloat16 [1024, 1024], replicated, may hold values from -0.1875 to 0.1875
- split_gain: float32 [1024], replicated, may hold values from 0.5 to 1.5
- split_shift: float32 [1024], replicated, may hold values from -2 to 2
- inner_kernel: bfloat16 [512, 512], replicated, may hold values from -0.25 to 0.25
- inner_gain: float32 [512], replicated, may hold values from 0.5 to 1.5
- inner_shift: float32 [512], replicated, may hold values from -2 to 2
- spread_kernel: bfloat16 [3, 3, 512, 512], replicated, may hold values from -0.09375 to 0.09375
- spread_gain: float32 [512], replicated, may hold values from 0.5 to 1.5
- spread_shift: float32 [512], replicated, may hold values from -2 to 2
- transition_kernel: bfloat16 [512, 512], replicated, may hold values from -0.25 to 0.25
- transition_gain: float32 [512], replicated, may hold values from 0.5 to 1.5
- transition_shift: float32 [512], replicated, may hold values from -2 to 2
- output_kernel: bfloat16 [1024, 1024], replicated, may hold values from -0.1875 to 0.1875
- output_gain: float32 [1024], replicated, may hold values from 0.5 to 1.5
- output_shift: float32 [1024], replicated, may hold values from -2 to 2
- cotangent: float32 [128, 19, 19, 1024], P(('dp', 'bn')), may hold values from -6 to 6
Outputs:
- result_map: float32 [128, 19, 19, 1024], P(('dp', 'bn'))
- grad_features: float32 [128, 19, 19, 1024], P(('dp', 'bn'))
- grad_split_kernel: float32 [1024, 1024], replicated
- grad_split_gain: float32 [1024], replicated
- grad_split_shift: float32 [1024], replicated
- grad_inner_kernel: float32 [512, 512], replicated
- grad_inner_gain: float32 [512], replicated
- grad_inner_shift: float32 [512], replicated
- grad_spread_kernel: float32 [3, 3, 512, 512], replicated
- grad_spread_gain: float32 [512], replicated
- grad_spread_shift: float32 [512], replicated
- grad_transition_kernel: float32 [512, 512], replicated
- grad_transition_gain: float32 [512], replicated
- grad_transition_shift: float32 [512], replicated
- grad_output_kernel: float32 [1024, 1024], replicated
- grad_output_gain: float32 [1024], replicated
- grad_output_shift: float32 [1024], replicated
Inputs may be any that keep to these rules, and one draw needn't show every extreme that they name: `image_counts`: each device has at least 2 live slots; some device has all 4. `map_sides`: each slot's side is 19, 16 or 13; sides of slots that are not live are to be ignored.
All inputs are finite; a program needn't handle non-finite values.
Results may differ from a plain program's by a relative error of at most 0.0003.
Values sent between devices are 32-bit elements; how exact they have to be, the bound alone decides.
A program may use at most 192 MiB of HBM per device.

v0:
```python
import jax
import jax.numpy as jnp
from jax import lax
from jax.sharding import PartitionSpec as P

SLOTS = 4
MAP = 19
epsilon = 1e-05


def mish(value):
    return value * jnp.tanh(jax.nn.softplus(value))


def convolve(inputs, kernel):
    return lax.conv_general_dilated(
        inputs,
        kernel,
        (1, 1),
        ((1, 1), (1, 1)),
        dimension_numbers=("NHWC", "HWIO", "NHWC"),
        precision=lax.Precision.HIGHEST,
    )


def pointwise(inputs, kernel):
    return jnp.einsum("nhwc,cd->nhwd", inputs, kernel, precision=lax.Precision.HIGHEST)


def kernel_grad(inputs, grad_z):
    return jnp.einsum("nhwc,nhwd->cd", inputs, grad_z, precision=lax.Precision.HIGHEST)


def masks(count_list, side_list):
    image = jnp.arange(side_list.shape[0])
    live = image % SLOTS < count_list[image // SLOTS]
    places = jnp.arange(MAP)
    inside = places[None, :] < side_list[:, None]
    keep = live[:, None, None] & inside[:, :, None] & inside[:, None, :]
    return keep.astype(jnp.float32)[..., None]


def local_sums(z, mask):
    return (jnp.sum(z * mask, axis=(0, 1, 2)), jnp.sum(z * z * mask, axis=(0, 1, 2)))


def finish(z, gain, shift, mask, first_sum, second_sum, total):
    mean = first_sum / total
    square = second_sum / total
    inverse_std = lax.rsqrt(square - mean * mean + epsilon)
    scaled = (z - mean) * inverse_std
    before = gain * scaled + shift
    return (mish(before) * mask, (scaled, inverse_std, before))


def norm_forward(z, gain, shift, mask, total):
    first_sum, second_sum = local_sums(z, mask)
    first_sum, second_sum = lax.psum((first_sum, second_sum), "bn")
    return finish(z, gain, shift, mask, first_sum, second_sum, total)


def norm_backward(grad_act, kept, gain, mask, total):
    scaled, inverse_std, before = kept
    unused, mish_pull = jax.vjp(mish, before)
    grad_before = mish_pull(grad_act * mask)[0]
    local_shift = jnp.sum(grad_before, axis=(0, 1, 2))
    local_gain = jnp.sum(grad_before * scaled, axis=(0, 1, 2))
    sum_shift, sum_gain = lax.psum((local_shift, local_gain), "bn")
    grad_z = mask * gain * inverse_std * (grad_before - (sum_shift + scaled * sum_gain) / total)
    return (grad_z, local_gain, local_shift)


def settle(kernel_part, gain_part, shift_part):
    return (kernel_part, gain_part, shift_part)


def local(
    features,
    image_counts,
    map_sides,
    split_kernel,
    split_gain,
    split_shift,
    inner_kernel,
    inner_gain,
    inner_shift,
    spread_kernel,
    spread_gain,
    spread_shift,
    transition_kernel,
    transition_gain,
    transition_shift,
    output_kernel,
    output_gain,
    output_shift,
    cotangent,
):
    half = inner_kernel.shape[0]
    split_weight = split_kernel.astype(jnp.float32)
    inner_weight = inner_kernel.astype(jnp.float32)
    spread_weight = spread_kernel.astype(jnp.float32)
    transition_weight = transition_kernel.astype(jnp.float32)
    output_weight = output_kernel.astype(jnp.float32)
    mask = masks(image_counts, map_sides)
    masked = features.astype(jnp.float32) * mask
    split_z = pointwise(masked, split_weight)
    first_sum, second_sum = local_sums(split_z, mask)
    first_sum, second_sum, total = lax.psum((first_sum, second_sum, jnp.sum(mask)), "bn")
    split, split_kept = finish(split_z, split_gain, split_shift, mask, first_sum, second_sum, total)
    part = split[..., :half]
    main = split[..., half:]
    inner, inner_kept = norm_forward(
        pointwise(main, inner_weight), inner_gain, inner_shift, mask, total
    )
    branch, spread_kept = norm_forward(
        convolve(inner, spread_weight), spread_gain, spread_shift, mask, total
    )
    joined = main + branch
    trans, trans_kept = norm_forward(
        pointwise(joined, transition_weight), transition_gain, transition_shift, mask, total
    )
    stacked = jnp.concatenate([trans, part], axis=-1)
    result, output_kept = norm_forward(
        pointwise(stacked, output_weight), output_gain, output_shift, mask, total
    )
    grad_z, gain_part, shift_part = norm_backward(cotangent, output_kept, output_gain, mask, total)
    grad_stacked = pointwise(grad_z, output_weight.T)
    output_grads = settle(kernel_grad(stacked, grad_z), gain_part, shift_part)
    grad_trans = grad_stacked[..., :half]
    grad_part = grad_stacked[..., half:]
    grad_z, gain_part, shift_part = norm_backward(
        grad_trans, trans_kept, transition_gain, mask, total
    )
    grad_joined = pointwise(grad_z, transition_weight.T)
    transition_grads = settle(kernel_grad(joined, grad_z), gain_part, shift_part)
    grad_z, gain_part, shift_part = norm_backward(
        grad_joined, spread_kept, spread_gain, mask, total
    )
    unused, spread_pull = jax.vjp(convolve, inner, spread_weight)
    grad_inner, grad_spread = spread_pull(grad_z)
    spread_grads = settle(grad_spread, gain_part, shift_part)
    grad_z, gain_part, shift_part = norm_backward(grad_inner, inner_kept, inner_gain, mask, total)
    grad_main = grad_joined + pointwise(grad_z, inner_weight.T)
    inner_grads = settle(kernel_grad(main, grad_z), gain_part, shift_part)
    grad_split = jnp.concatenate([grad_part, grad_main], axis=-1)
    grad_z, gain_part, shift_part = norm_backward(grad_split, split_kept, split_gain, mask, total)
    grad_features = pointwise(grad_z, split_weight.T) * mask
    split_grads = settle(kernel_grad(masked, grad_z), gain_part, shift_part)
    summed = lax.psum(
        (
            split_grads[0],
            split_grads[1],
            split_grads[2],
            inner_grads[0],
            inner_grads[1],
            inner_grads[2],
            spread_grads[0],
            spread_grads[1],
            spread_grads[2],
            transition_grads[0],
            transition_grads[1],
            transition_grads[2],
            output_grads[0],
            output_grads[1],
            output_grads[2],
        ),
        ("dp", "bn"),
    )
    return (
        result,
        grad_features,
        summed[0],
        summed[1],
        summed[2],
        summed[3],
        summed[4],
        summed[5],
        summed[6],
        summed[7],
        summed[8],
        summed[9],
        summed[10],
        summed[11],
        summed[12],
        summed[13],
        summed[14],
    )


def solution(mesh):
    return jax.shard_map(
        local,
        mesh=mesh,
        in_specs=(
            P(("dp", "bn"), None, None, None),
            P(("dp", "bn")),
            P(("dp", "bn")),
            P(),
            P(),
            P(),
            P(),
            P(),
            P(),
            P(),
            P(),
            P(),
            P(),
            P(),
            P(),
            P(),
            P(),
            P(),
            P(("dp", "bn"), None, None, None),
        ),
        out_specs=(
            P(("dp", "bn"), None, None, None),
            P(("dp", "bn"), None, None, None),
            P(),
            P(),
            P(),
            P(),
            P(),
            P(),
            P(),
            P(),
            P(),
            P(),
            P(),
            P(),
            P(),
            P(),
            P(),
        ),
        check_vma=False,
    )
```

profile of v0, /device:TPU:0, one launch (start us, length us, event | category | flops | bytes accessed | tf_op | source)
XLA Modules:
  0.0 992.0 jit_solution(5745738842142313879)
XLA Ops:
  9.7 19.9 %multiply_reduce_fusion.5 = (f32[1024]{0:T(1024)S(1)}, f32[1024]{0:T(1024)S(1)}, f32[4,19,19,1024]{3,2,1,0:T(8,128)}, f32[4,19,19,1024]{3,2,1,0:T(8,128)}) fusion(f32[4,19,19]{2,1,0:T(8,128)S(1)} %and_convert_fusion, bf16[4,19,19,1024]{3,0,2,1:T(4,128)(2,1)} %param.21, bf16[1024,1024]{1,0:T(8,128)(2,1)S(1)} %copy-done), kind=kOutput, calls=%fused_computation.52 | convolution fusion | flops 18183030784 | bytes 16897680 | tf_op jit(solution)/shard_map/nhwc,cd->nhwd/dot_general | solution.py:27
  29.6 9.3 all-reduce.11
  39.5 7.8 fusion.14
  47.4 5.4 multiply_reduce_fusion.11
  52.8 6.0 all-reduce.10
  59.4 4.5 fusion.117
  64.0 4.1 fusion.54
  71.8 4.2 select_maximum_fusion.1
  76.0 43.0 %fusion.109 = (f32[19,32,3,512]{3,1,2,0:T(8,128)S(1)}, f32[19,32,3,512]{3,1,2,0:T(8,128)}) fusion(bf16[3,3,512,512]{3,2,1,0:T(8,128)(2,1)} %param.30, f32[19,4,8,5,512]{4,1,3,2,0:T(4,128)} %select_maximum_fusion.1, pred[32,3]{0,1:T(4,128)(4,1)S(1)} %copy-done.70), kind=kOutput, calls=%fused_computation.176 | convolution fusion | flops 49830199296 | bytes 18415712 | tf_op jit(solution)/shard_map/conv_general_dilated | solution.py:16
  119.1 4.9 copy.90
  123.9 7.0 reshape.143
  131.0 6.9 copy.88
  137.9 7.0 reshape.141
  144.9 3.6 fusion.46
  148.5 5.9 all-reduce.9
  155.1 7.8 fusion.23
  162.9 4.9 copy.92
  167.7 7.0 reshape.147
  174.8 6.9 fusion.108
  181.8 5.3 multiply_reduce_fusion.9
  187.1 6.0 all-reduce.8
  193.8 4.5 fusion.55
  198.3 14.4 %multiply_reduce_fusion.3 = (f32[1024]{0:T(1024)S(1)}, f32[1024]{0:T(1024)S(1)}, f32[4,19,19,1024]{3,2,1,0:T(8,128)}) fusion(f32[4,19,19]{2,1,0:T(8,128)S(1)} %and_convert_fusion, bf16[1024,1024]{1,0:T(8,128)(2,1)S(1)} %copy-done.66, f32[4,19,19,512]{3,2,1,0:T(8,128)S(1)} %copy-done.16, f32[4,19,19,512]{3,2,1,0:T(8,128)S(1)} %fusion.55), kind=kOutput, calls=%fused_computation.47 | convolution fusion | flops 18178594816 | bytes 13940368 | tf_op jit(solution)/shard_map/nhwc,cd->nhwd/dot_general | solution.py:27
  212.7 6.8 all-reduce.7
  220.1 17.3 %fusion.100 = (f32[1024]{0:T(1024)S(1)}, f32[1024]{0:T(1024)S(1)}, f32[4,19,19,1024]{3,2,1,0:T(8,128)}, f32[4,19,19,1024]{3,2,1,0:T(8,128)}) fusion(f32[1024]{0:T(1024)S(1)} %get-tuple-element.159, f32[4,19,19,1024]{3,2,1,0:T(8,128)} %get-tuple-element.175, f32[1024]{0:T(1024)S(1)} %get-tuple-element.158, f32[1024]{0:T(1024)S(1)} %copy-done.64, ...), kind=kLoop, calls=%fused_computation.172 | loop fusion | flops 42878976 | bytes 23688848 | tf_op jit(solution)/shard_map/reduce_sum | solution.py:66
  237.5 5.8 all-reduce.6
  243.3 7.3 subtract_multiply_fusion.1
  250.6 13.9 %fusion.72 = f32[4,19,19,1024]{3,2,1,0:T(8,128)} fusion(f32[4,19,19,1024]{3,2,1,0:T(8,128)S(1)} %subtract_multiply_fusion.1, bf16[1024,1024]{1,0:T(8,128)(2,1)S(1)} %copy-done.67), kind=kOutput, calls=%fused_computation.135 | convolution fusion | flops 18169724928 | bytes 13926400 | tf_op jit(solution)/shard_map/nhwc,cd->nhwd/dot_general | solution.py:27
  264.5 28.9 %fusion.64 = f32[1024,1024]{1,0:T(8,128)} fusion(f32[4,19,19,1024]{3,2,1,0:T(8,128)S(1)} %subtract_multiply_fusion.1, f32[4,19,19,512]{3,2,1,0:T(8,128)S(1)} %copy-done.17, f32[4,19,19,512]{3,2,1,0:T(8,128)S(1)} %copy-done.21), kind=kOutput, calls=%fused_computation.131 | convolution fusion | flops 18171203584 | bytes 16023552 | tf_op jit(solution)/shard_map/nhwc,nhwd->cd/dot_general | solution.py:31
  293.5 4.9 copy.97
  298.3 7.1 reshape.156
  305.4 6.9 copy.95
  312.3 7.0 reshape.145
  319.4 9.4 fusion.102
  328.8 6.6 all-reduce.5
  335.4 18.8 %fusion.85 = f32[512,512]{1,0:T(8,128)} fusion(f32[4,19,19,512]{3,2,1,0:T(8,128)} %copy-done.6, f32[4,19,19,512]{3,2,1,0:T(8,128)} %get-tuple-element.147, f32[4,19,19,512]{3,2,1,0:T(8,128)} %get-tuple-element.174, f32[]{:T(128)} %get-tuple-element.142, f32[512]{0:T(512)S(1)} %get-tuple-element.129, f32[512]{0:T(512)S(1)} %get-tuple-element.130, ...), kind=kOutput, calls=%fused_computation.143 | convolution fusion | flops 4549085184 | bytes 9936532 | tf_op jit(solution)/shard_map/nhwc,nhwd->cd/dot_general | solution.py:31
  354.3 10.6 %fusion.40 = (f32[512]{0:T(512)S(1)}, f32[512]{0:T(512)S(1)}, f32[4,19,19,512]{3,2,1,0:T(8,128)}, f32[4,19,19,512]{3,2,1,0:T(8,128)}) fusion(f32[4,19,19]{2,1,0:T(8,128)S(1)} %and_convert_fusion, bf16[512,512]{1,0:T(8,128)(2,1)S(1)} %copy-done.27, f32[19,4,24,512]{3,2,1,0:T(8,128)S(1)} %copy-done.23, f32[19,4,24,512]{3,2,1,0:T(8,128)S(1)} %copy-done.24, ...), kind=kOutput, calls=%fused_computation.85 | convolution fusion | flops 4566088704 | bytes 21493764 | tf_op jit(solution)/shard_map/nhwc,cd->nhwd/dot_general | solution.py:27
  364.8 5.8 all-reduce.4
  370.7 3.2 add_divide_fusion
  373.9 4.9 copy.99
  378.7 7.0 reshape.158
  385.8 3.8 fusion.38
  393.4 4.4 select_maximum_fusion
  397.8 34.3 %broadcast_select_fusion = f32[19,32,3,512]{3,1,2,0:T(8,128)S(1)} fusion(pred[32,3]{0,1:T(4,128)(4,1)S(1)} %copy-done.70, bf16[3,3,512,512]{3,2,1,0:T(8,128)(2,1)} %param.30, f32[19,4,8,5,512]{4,1,3,2,0:T(4,128)} %select_maximum_fusion), kind=kOutput, calls=%fused_computation.140 | convolution fusion | flops 49829265408 | bytes 14680160 | tf_op jit(solution)/shard_map/transpose(jvp())/conv_general_dilated | solution.py:16
  432.1 4.9 copy.103
  437.0 7.1 reshape.154
  444.1 8.4 fusion.101
  452.5 6.6 all-reduce.3
  459.2 11.2 %convolution_add_fusion = f32[4,19,19,512]{3,2,1,0:T(8,128)} fusion(f32[4,19,19,512]{3,2,1,0:T(8,128)} %get-tuple-element.176, bf16[512,512]{1,0:T(8,128)(2,1)S(1)} %copy-done.69, f32[4,19,19,512]{3,2,1,0:T(8,128)} %get-tuple-element.145, f32[4,19,19,512]{3,2,1,0:T(8,128)} %get-tuple-element.171, f32[512]{0:T(512)S(1)} %get-tuple-element.125, ...), kind=kOutput, calls=%fused_computation.139 | convolution fusion | flops 4549824512 | bytes 12369556 | tf_op jit(solution)/shard_map/nhwc,cd->nhwd/dot_general | solution.py:27
  470.4 10.2 %fusion.80 = f32[512,512]{1,0:T(8,128)} fusion(f32[4,19,19,512]{3,2,1,0:T(8,128)S(1)} %copy-done.15, f32[4,19,19,512]{3,2,1,0:T(8,128)S(1)} %copy-done.22, f32[4,19,19,512]{3,2,1,0:T(8,128)S(1)} %copy-done.2, f32[512]{0:T(512)S(1)} %get-tuple-element.125, f32[512]{0:T(512)S(1)} %get-tuple-element.126, f32[]{:T(128)} %get-tuple-element.142, ...), kind=kOutput, calls=%fused_computation.142 | convolution fusion | flops 4549085184 | bytes 9936532 | tf_op jit(solution)/shard_map/nhwc,nhwd->cd/dot_general | solution.py:31
  480.7 108.9 %fusion.56 = f32[3,3,512,512]{3,2,1,0:T(8,128)} fusion(f32[4,19,19,512]{3,2,1,0:T(8,128)S(1)} %copy-done.9, f32[4,19,19,512]{3,2,1,0:T(8,128)S(1)} %copy-done.19), kind=kOutput, calls=%fused_computation.127 | convolution fusion | flops 38063308800 | bytes 15351808 | tf_op jit(solution)/shard_map/transpose(jvp())/conv_general_dilated | solution.py:16
  589.7 12.9 %fusion.99 = (f32[1024]{0:T(1024)S(1)}, f32[1024]{0:T(1024)S(1)}, f32[4,19,19,1024]{3,2,1,0:T(8,128)}) fusion(f32[1024]{0:T(1024)S(1)} %copy-done.31, f32[4,19,19,1024]{3,2,1,0:T(8,128)} %get-tuple-element.170, f32[1024]{0:T(1024)S(1)} %copy-done.29, f32[1024]{0:T(1024)S(1)} %copy-done.55, f32[1024]{0:T(1024)S(1)} %copy-done.37, ...), kind=kLoop, calls=%fused_computation.171 | loop fusion | flops 41400320 | bytes 17774224 | tf_op jit(solution)/shard_map/reduce_sum | solution.py:66
  602.6 5.7 all-reduce.2
  608.3 7.4 subtract_multiply_fusion
  615.7 3.0 copy-done.13
  618.7 28.9 %fusion.59 = f32[1024,1024]{1,0:T(8,128)} fusion(f32[4,19,19,1024]{3,2,1,0:T(8,128)S(1)} %subtract_multiply_fusion, f32[4,19,19,1024]{3,2,1,0:T(8,128)S(1)} %copy-done.71), kind=kOutput, calls=%fused_computation.130 | convolution fusion | flops 18169724928 | bytes 16023552 | tf_op jit(solution)/shard_map/nhwc,nhwd->cd/dot_general | solution.py:31
  647.7 10.0 %copy.115 = f32[4,19,19,1024]{3,0,2,1:T(4,128)} copy(f32[4,19,19,1024]{3,2,1,0:T(8,128)} %get-tuple-element.152) | data formatting | bytes 11829248
  657.7 14.8 %broadcast_multiply_fusion = f32[4,19,19,1024]{3,2,1,0:T(8,128)S(1)} fusion(f32[4,19,19]{2,1,0:T(8,128)S(1)} %copy-done.11, f32[4,19,19,1024]{3,2,1,0:T(8,128)} %copy-done.13, bf16[1024,1024]{1,0:T(8,128)(2,1)S(1)} %copy-done), kind=kOutput, calls=%fused_computation.126 | convolution fusion | flops 18171203584 | bytes 13932176 | tf_op jit(solution)/shard_map/nhwc,cd->nhwd/dot_general | solution.py:27
  672.6 6.9 copy.116
  679.6 42.0 %all-reduce = (f32[1024]{0:T(1024)}, f32[1024]{0:T(1024)}, f32[512]{0:T(512)}, f32[512]{0:T(512)}, f32[512]{0:T(512)}, /*index=5*/f32[512]{0:T(512)}, f32[512]{0...) all-reduce(f32[1024]{0:T(1024)S(1)} %get-tuple-element.93, ...), channel_id=1, replica_groups=mesh['dp'=8,'bn'=4] {'dp','bn'}, use_global_device_ids=true, to_apply=%region_43.46 | all-reduce | flops 7168 | bytes 57344 | tf_op jit(solution)/shard_map/psum | solution.py:149
  721.6 247.1 %all-reduce.14.cloned.1.call-done = (f32[1024,1024]{1,0:T(8,128)}, f32[512,512]{1,0:T(8,128)}, f32[3,3,512,512]{3,2,1,0:T(8,128)}, f32[512,512]{1,0:T(8,128)}, f32[1024,1024]{1,0:T(8,128)}) async-done(((f32[1024,1024]{1,0:T(8,128)}, f32[512,512]{1,0:T(8,128)}, f32[3,3,512,512]{3,2,1,0:T(8,128)}, f32[512,512]{1,0:T(8,128)}, f32[1024,1024]{1,0:T(8,128)}), (f32[1024,1024]{1,0:T(8,128)}, f32[512,512]{1,0:T(8,128)}, ...) | async-done | bytes 19922960 | tf_op jit(solution)/shard_map/psum | solution.py:149
  968.6 5.1 copy.233
  973.7 2.7 copy.234
  976.4 4.8 copy.235
  (163 shorter events, 16.0 us)
Async XLA Ops:
  7.2 961.4 %all-reduce.14.cloned.1.call-start = ((), (), s32[]{:S(2)}) async-start(), calls=%async_computation | async-start | bytes 39845888 | tf_op jit(solution)/shard_map/psum | solution.py:149
  9.0 461.4 %copy-start.10 = (f32[4,19,19]{2,1,0:T(8,128)}, f32[4,19,19]{2,1,0:T(8,128)S(1)}, u32[]{:S(2)}) copy-start(f32[4,19,19]{2,1,0:T(8,128)S(1)} %and_convert_fusion) | copy-start | bytes 17332
  9.7 29.8 %copy-start.36 = (f32[1024]{0:T(1024)S(1)}, f32[1024]{0:T(1024)}, u32[]{:S(2)}) copy-start(f32[1024]{0:T(1024)} %param.25) | copy-start | bytes 12292
  9.7 29.8 %copy-start.54 = (f32[1024]{0:T(1024)S(1)}, f32[1024]{0:T(1024)}, u32[]{:S(2)}) copy-start(f32[1024]{0:T(1024)} %param.26) | copy-start | bytes 12292
  39.5 7.9 copy-start.28
  39.5 7.9 copy-start.30
  39.5 7.8 copy-start.68
  47.4 5.4 copy-start.5
  47.4 12.0 %copy-start.42 = (f32[512]{0:T(512)S(1)}, f32[512]{0:T(512)}, u32[]{:S(2)}) copy-start(f32[512]{0:T(512)} %param.29) | copy-start | bytes 6148
  47.4 12.0 %copy-start.44 = (f32[512]{0:T(512)S(1)}, f32[512]{0:T(512)}, u32[]{:S(2)}) copy-start(f32[512]{0:T(512)} %param.28) | copy-start | bytes 6148
  144.9 10.1 %copy-start.59 = (f32[512]{0:T(512)S(1)}, f32[512]{0:T(512)}, u32[]{:S(2)}) copy-start(f32[512]{0:T(512)} %param.31) | copy-start | bytes 6148
  144.9 10.1 %copy-start.65 = (f32[512]{0:T(512)S(1)}, f32[512]{0:T(512)}, u32[]{:S(2)}) copy-start(f32[512]{0:T(512)} %param.32) | copy-start | bytes 6148
  174.8 6.9 copy-start.27
  181.7 5.4 copy-start.6
  181.7 12.0 %copy-start.57 = (f32[512]{0:T(512)S(1)}, f32[512]{0:T(512)}, u32[]{:S(2)}) copy-start(f32[512]{0:T(512)} %param.35) | copy-start | bytes 6148
  181.7 12.0 %copy-start.58 = (f32[512]{0:T(512)S(1)}, f32[512]{0:T(512)}, u32[]{:S(2)}) copy-start(f32[512]{0:T(512)} %param.34) | copy-start | bytes 6148
  198.3 14.4 %copy-start.20 = (f32[4,19,19,512]{3,2,1,0:T(8,128)}, f32[4,19,19,512]{3,2,1,0:T(8,128)S(1)}, u32[]{:S(2)}) copy-start(f32[4,19,19,512]{3,2,1,0:T(8,128)S(1)} %fusion.55) | copy-start | bytes 8871940
  198.3 21.8 %copy-start.56 = (f32[1024]{0:T(1024)S(1)}, f32[1024]{0:T(1024)}, u32[]{:S(2)}) copy-start(f32[1024]{0:T(1024)} %param.37) | copy-start | bytes 12292
  198.3 21.8 %copy-start.64 = (f32[1024]{0:T(1024)S(1)}, f32[1024]{0:T(1024)}, u32[]{:S(2)}) copy-start(f32[1024]{0:T(1024)} %param.38) | copy-start | bytes 12292
  237.5 13.1 %copy-start.32 = (f32[1024]{0:T(1024)}, f32[1024]{0:T(1024)S(1)}, u32[]{:S(2)}) copy-start(f32[1024]{0:T(1024)S(1)} %get-tuple-element.94) | copy-start | bytes 12292
  237.5 13.1 %copy-start.34 = (f32[1024]{0:T(1024)}, f32[1024]{0:T(1024)S(1)}, u32[]{:S(2)}) copy-start(f32[1024]{0:T(1024)S(1)} %get-tuple-element.95) | copy-start | bytes 12292
  243.3 7.3 copy-start.67
  250.6 13.9 %copy-start.17 = (f32[4,19,19,512]{3,2,1,0:T(8,128)S(1)}, f32[4,19,19,512]{3,2,1,0:T(8,128)}, u32[]{:S(2)}) copy-start(f32[4,19,19,512]{3,2,1,0:T(8,128)} %get-tuple-element.155) | copy-start | bytes 8871940
  250.6 13.9 %copy-start.21 = (f32[4,19,19,512]{3,2,1,0:T(8,128)S(1)}, f32[4,19,19,512]{3,2,1,0:T(8,128)}, u32[]{:S(2)}) copy-start(f32[4,19,19,512]{3,2,1,0:T(8,128)} %copy-done.20) | copy-start | bytes 8871940
  264.5 28.9 %copy-start.3 = (f32[19,32,3,512]{3,1,2,0:T(8,128)S(1)}, f32[19,32,3,512]{3,1,2,0:T(8,128)}, u32[]{:S(2)}) copy-start(f32[19,32,3,512]{3,1,2,0:T(8,128)} %get-tuple-element.151) | copy-start | bytes 11206660
  328.8 25.4 %copy-start.46 = (f32[512]{0:T(512)}, f32[512]{0:T(512)S(1)}, u32[]{:S(2)}) copy-start(f32[512]{0:T(512)S(1)} %get-tuple-element.104) | copy-start | bytes 6148
  328.8 25.4 %copy-start.48 = (f32[512]{0:T(512)}, f32[512]{0:T(512)S(1)}, u32[]{:S(2)}) copy-start(f32[512]{0:T(512)S(1)} %get-tuple-element.105) | copy-start | bytes 6148
  335.4 18.8 %copy-start.4 = (f32[4,19,19,512]{3,2,1,0:T(8,128)S(1)}, f32[4,19,19,512]{3,2,1,0:T(8,128)}, u32[]{:S(2)}) copy-start(f32[4,19,19,512]{3,2,1,0:T(8,128)} %get-tuple-element.174) | copy-start | bytes 8871940
  335.4 18.8 %copy-start.23 = (f32[19,4,24,512]{3,2,1,0:T(8,128)S(1)}, f32[19,4,24,512]{3,2,1,0:T(8,128)}, u32[]{:S(2)}) copy-start(f32[19,4,24,512]{3,2,1,0:T(8,128)} %reshape.156) | copy-start | bytes 11206660
  335.4 18.8 %copy-start.24 = (f32[19,4,24,512]{3,2,1,0:T(8,128)S(1)}, f32[19,4,24,512]{3,2,1,0:T(8,128)}, u32[]{:S(2)}) copy-start(f32[19,4,24,512]{3,2,1,0:T(8,128)} %reshape.145) | copy-start | bytes 11206660
  335.4 18.8 %copy-start.25 = (f32[4,19,19,512]{3,2,1,0:T(8,128)S(1)}, f32[4,19,19,512]{3,2,1,0:T(8,128)}, u32[]{:S(2)}) copy-start(f32[4,19,19,512]{3,2,1,0:T(8,128)} %get-tuple-element.147) | copy-start | bytes 8871940
  364.8 9.0 copy-start.60
  364.8 9.0 copy-start.62
  437.0 7.1 copy-start.39
  437.0 7.1 copy-start.41
  437.0 7.1 copy-start.43
  437.0 7.1 copy-start.45
  444.1 15.0 %copy-start.69 = (bf16[512,512]{1,0:T(8,128)(2,1)S(1)}, bf16[512,512]{1,0:T(8,128)(2,1)}, u32[]{:S(2)}) copy-start(bf16[512,512]{1,0:T(8,128)(2,1)} %param.27) | copy-start | bytes 1572868
  452.5 17.8 %copy-start.50 = (f32[512]{0:T(512)}, f32[512]{0:T(512)S(1)}, u32[]{:S(2)}) copy-start(f32[512]{0:T(512)S(1)} %get-tuple-element.100) | copy-start | bytes 6148
  452.5 17.8 %copy-start.52 = (f32[512]{0:T(512)}, f32[512]{0:T(512)S(1)}, u32[]{:S(2)}) copy-start(f32[512]{0:T(512)S(1)} %get-tuple-element.101) | copy-start | bytes 6148
  459.1 11.2 %copy-start.2 = (f32[4,19,19,512]{3,2,1,0:T(8,128)S(1)}, f32[4,19,19,512]{3,2,1,0:T(8,128)}, u32[]{:S(2)}) copy-start(f32[4,19,19,512]{3,2,1,0:T(8,128)} %get-tuple-element.171) | copy-start | bytes 8871940
  459.1 11.2 %copy-start.15 = (f32[4,19,19,512]{3,2,1,0:T(8,128)S(1)}, f32[4,19,19,512]{3,2,1,0:T(8,128)}, u32[]{:S(2)}) copy-start(f32[4,19,19,512]{3,2,1,0:T(8,128)} %get-tuple-element.153) | copy-start | bytes 8871940
  459.1 11.2 %copy-start.22 = (f32[4,19,19,512]{3,2,1,0:T(8,128)S(1)}, f32[4,19,19,512]{3,2,1,0:T(8,128)}, u32[]{:S(2)}) copy-start(f32[4,19,19,512]{3,2,1,0:T(8,128)} %get-tuple-element.145) | copy-start | bytes 8871940
  470.4 10.2 %copy-start.9 = (f32[4,19,19,512]{3,2,1,0:T(8,128)S(1)}, f32[4,19,19,512]{3,2,1,0:T(8,128)}, u32[]{:S(2)}) copy-start(f32[4,19,19,512]{3,2,1,0:T(8,128)} %copy-done.8) | copy-start | bytes 8871940
  470.4 10.2 %copy-start.19 = (f32[4,19,19,512]{3,2,1,0:T(8,128)S(1)}, f32[4,19,19,512]{3,2,1,0:T(8,128)}, u32[]{:S(2)}) copy-start(f32[4,19,19,512]{3,2,1,0:T(8,128)} %fusion.54) | copy-start | bytes 8871940
  480.6 109.0 %copy-start.7 = (f32[4,19,19,512]{3,2,1,0:T(8,128)S(1)}, f32[4,19,19,512]{3,2,1,0:T(8,128)}, u32[]{:S(2)}) copy-start(f32[4,19,19,512]{3,2,1,0:T(8,128)} %get-tuple-element.156) | copy-start | bytes 8871940
  480.6 109.0 %copy-start.11 = (f32[4,19,19]{2,1,0:T(8,128)S(1)}, f32[4,19,19]{2,1,0:T(8,128)}, u32[]{:S(2)}) copy-start(f32[4,19,19]{2,1,0:T(8,128)} %copy-done.10) | copy-start | bytes 17332
  480.6 109.0 %copy-start.18 = (f32[4,19,19,512]{3,2,1,0:T(8,128)S(1)}, f32[4,19,19,512]{3,2,1,0:T(8,128)}, u32[]{:S(2)}) copy-start(f32[4,19,19,512]{3,2,1,0:T(8,128)} %convolution_add_fusion) | copy-start | bytes 8871940
  480.6 109.0 %copy-start.29 = (f32[1024]{0:T(1024)S(1)}, f32[1024]{0:T(1024)}, u32[]{:S(2)}) copy-start(f32[1024]{0:T(1024)} %copy-done.28) | copy-start | bytes 12292
  480.6 109.0 %copy-start.31 = (f32[1024]{0:T(1024)S(1)}, f32[1024]{0:T(1024)}, u32[]{:S(2)}) copy-start(f32[1024]{0:T(1024)} %copy-done.30) | copy-start | bytes 12292
  480.6 109.0 %copy-start.37 = (f32[1024]{0:T(1024)S(1)}, f32[1024]{0:T(1024)}, u32[]{:S(2)}) copy-start(f32[1024]{0:T(1024)} %param.25) | copy-start | bytes 12292
  480.6 109.0 %copy-start.55 = (f32[1024]{0:T(1024)S(1)}, f32[1024]{0:T(1024)}, u32[]{:S(2)}) copy-start(f32[1024]{0:T(1024)} %param.26) | copy-start | bytes 12292
  608.3 10.4 %copy-start.71 = (f32[4,19,19,1024]{3,2,1,0:T(8,128)S(1)}, f32[4,19,19,1024]{3,2,1,0:T(8,128)}, u32[]{:S(2)}) copy-start(f32[4,19,19,1024]{3,2,1,0:T(8,128)} %get-tuple-element.157) | copy-start | bytes 17743876
  672.5 7.0 copy-start.33
  672.5 7.0 copy-start.35
  672.5 7.0 copy-start.47
  672.5 7.0 copy-start.49
  672.6 7.0 copy-start.51
  672.6 7.0 copy-start.53
  672.6 7.0 copy-start.61
  672.6 7.0 copy-start.63
  968.6 7.7 copy-start.12
  976.4 4.8 copy-start.26
  976.4 6.3 copy-start.14
  (9 other events, 35.8 us)
Sparse Core Ops, SparseCore 0:
  647.8 320.8 all-reduce.13
where the time goes:
time: 998 us; the launch traced here: 992 us
  matrix products  369 us (37%)
  waiting for transfers between devices  247 us (25%)
  local copies, waits for them, and re-layouts  131 us (13%)
  other arithmetic  122 us (12%)
  blocking collectives  107 us (11%)
  between operations  16.3 us (2%)
    psum x1, waiting for transfers between devices, local(): lax.psum((split_grads[0], split_grads[1], split_grads[2], inner_grads[0],...  247 us
    conv_general_dilated x3, matrix products, convolve(): lax.conv_general_dilated(inputs, kernel, (1, 1), ((1, 1), (1, 1)), dimens...  186 us
    dot_general x8, matrix products, pointwise(): jnp.einsum('nhwc,cd->nhwd', inputs, kernel, precision=lax.Precision.HIGHEST)  95.4 us
    dot_general x4, matrix products, kernel_grad(): jnp.einsum('nhwc,nhwd->cd', inputs, grad_z, precision=lax.Precision.HIGHEST)  86.9 us
    reduce_sum x4, other arithmetic, norm_backward(): local_shift = jnp.sum(grad_before, axis=(0, 1, 2))  48 us
    psum x1, blocking collectives, local(): lax.psum((split_grads[0], split_grads[1], split_grads[2], inner_grads[0],...  42 us
    unnamed x153, local copies, waits for them, and re-layouts  40.6 us
    psum x5, blocking collectives, norm_backward(): sum_shift, sum_gain = lax.psum((local_shift, local_gain), 'bn')  30.5 us
  transfers between devices with their start and end apart: 1, of which 1 were waited for; matrix products, arithmetic and copies ran while one was open for 3% of the time, Pallas kernels for 0%

commit v1 on v0

--- a/solution.py
+++ b/solution.py
@@ -146,26 +146,25 @@
     grad_z, gain_part, shift_part = norm_backward(grad_split, split_kept, split_gain, mask, total)
     grad_features = pointwise(grad_z, split_weight.T) * mask
     split_grads = settle(kernel_grad(masked, grad_z), gain_part, shift_part)
-    summed = lax.psum(
-        (
-            split_grads[0],
-            split_grads[1],
-            split_grads[2],
-            inner_grads[0],
-            inner_grads[1],
-            inner_grads[2],
-            spread_grads[0],
-            spread_grads[1],
-            spread_grads[2],
-            transition_grads[0],
-            transition_grads[1],
-            transition_grads[2],
-            output_grads[0],
-            output_grads[1],
-            output_grads[2],
-        ),
-        ("dp", "bn"),
-    )
+    summed = (
+        split_grads[0],
+        split_grads[1],
+        split_grads[2],
+        inner_grads[0],
+        inner_grads[1],
+        inner_grads[2],
+        spread_grads[0],
+        spread_grads[1],
+        spread_grads[2],
+        transition_grads[0],
+        transition_grads[1],
+        transition_grads[2],
+        output_grads[0],
+        output_grads[1],
+        output_grads[2],
+    )
+    for pp in ("bn", "dp"):
+        summed = lax.psum(summed, axis_name=pp)
     return (
         result,
         grad_features,

time: 998 us -> 1630 us (1.63)
  waiting for transfers between devices: 247 us -> 878 us
    psum x1 -> x2, waiting for transfers between devices: 247 us -> 878 us  [local(): summed = lax.psum(summed, axis_name=pp)]
  transfers between devices with their start and end apart: 1 -> 2, of which waited for: 1 -> 2; matrix products, arithmetic and copies ran while one was open for 3% -> 2% of each run, Pallas kernels for 0% -> 0%
where the time goes in v1:
time: 1630 us; the launch traced here: 1620 us
  waiting for transfers between devices  878 us (54%)
  matrix products  370 us (23%)
  local copies, waits for them, and re-layouts  131 us (8%)
  other arithmetic  123 us (8%)
  blocking collectives  105 us (6%)
  between operations  16.3 us (1%)
    psum x2, waiting for transfers between devices, local(): summed = lax.psum(summed, axis_name=pp)  878 us
    conv_general_dilated x3, matrix products, convolve(): lax.conv_general_dilated(inputs, kernel, (1, 1), ((1, 1), (1, 1)), dimens...  186 us
    dot_general x8, matrix products, pointwise(): jnp.einsum('nhwc,cd->nhwd', inputs, kernel, precision=lax.Precision.HIGHEST)  96.4 us
    dot_general x4, matrix products, kernel_grad(): jnp.einsum('nhwc,nhwd->cd', inputs, grad_z, precision=lax.Precision.HIGHEST)  87 us
    reduce_sum x4, other arithmetic, norm_backward(): local_shift = jnp.sum(grad_before, axis=(0, 1, 2))  47.9 us
    unnamed x153, local copies, waits for them, and re-layouts  40.5 us
    psum x1, blocking collectives, local(): summed = lax.psum(summed, axis_name=pp)  40.3 us
  transfers between devices with their start and end apart: 2, of which 2 were waited for; matrix products, arithmetic and copies ran while one was open for 2% of the time, Pallas kernels for 0%

profile of v1, /device:TPU:0, one launch (start us, length us, event | category | flops | bytes accessed | tf_op | source)
XLA Modules:
  0.0 1622.4 jit_solution(16651037444953404785)
XLA Ops:
  9.7 19.9 %multiply_reduce_fusion.5 = (f32[1024]{0:T(1024)S(1)}, f32[1024]{0:T(1024)S(1)}, f32[4,19,19,1024]{3,2,1,0:T(8,128)}, f32[4,19,19,1024]{3,2,1,0:T(8,128)}) fusion(f32[4,19,19]{2,1,0:T(8,128)S(1)} %and_convert_fusion, bf16[4,19,19,1024]{3,0,2,1:T(4,128)(2,1)} %param.21, bf16[1024,1024]{1,0:T(8,128)(2,1)S(1)} %copy-done), kind=kOutput, calls=%fused_computation.52 | convolution fusion | flops 18183030784 | bytes 16897680 | tf_op jit(solution)/shard_map/nhwc,cd->nhwd/dot_general | solution.py:27
  29.6 9.4 all-reduce.11
  39.6 7.8 fusion.14
  47.5 5.4 multiply_reduce_fusion.11
  52.9 6.0 all-reduce.10
  59.5 4.8 fusion.117
  64.4 4.1 fusion.54
  72.3 4.2 select_maximum_fusion.1
  76.5 43.0 %fusion.109 = (f32[19,32,3,512]{3,1,2,0:T(8,128)S(1)}, f32[19,32,3,512]{3,1,2,0:T(8,128)}) fusion(bf16[3,3,512,512]{3,2,1,0:T(8,128)(2,1)} %param.30, f32[19,4,8,5,512]{4,1,3,2,0:T(4,128)} %select_maximum_fusion.1, pred[32,3]{0,1:T(4,128)(4,1)S(1)} %copy-done.70), kind=kOutput, calls=%fused_computation.176 | convolution fusion | flops 49830199296 | bytes 18415712 | tf_op jit(solution)/shard_map/conv_general_dilated | solution.py:16
  119.6 4.9 copy.90
  124.4 7.0 reshape.143
  131.5 6.9 copy.88
  138.4 7.0 reshape.141
  145.4 3.6 fusion.46
  149.0 5.9 all-reduce.9
  155.6 7.8 fusion.23
  163.4 4.9 copy.92
  168.3 7.0 reshape.147
  175.3 6.9 fusion.108
  182.3 5.3 multiply_reduce_fusion.9
  187.6 6.0 all-reduce.8
  194.3 4.5 fusion.55
  198.9 14.4 multiply_reduce_fusion.3
  213.3 6.8 all-reduce.7
  220.7 17.2 %fusion.100 = (f32[1024]{0:T(1024)S(1)}, f32[1024]{0:T(1024)S(1)}, f32[4,19,19,1024]{3,2,1,0:T(8,128)}, f32[4,19,19,1024]{3,2,1,0:T(8,128)}) fusion(f32[1024]{0:T(1024)S(1)} %get-tuple-element.164, f32[4,19,19,1024]{3,2,1,0:T(8,128)} %get-tuple-element.180, f32[1024]{0:T(1024)S(1)} %get-tuple-element.163, f32[1024]{0:T(1024)S(1)} %copy-done.56, ...), kind=kLoop, calls=%fused_computation.172 | loop fusion | flops 42878976 | bytes 23688848 | tf_op jit(solution)/shard_map/reduce_sum | solution.py:66
  238.0 5.7 all-reduce.6
  243.8 7.3 subtract_multiply_fusion.1
  251.2 13.9 fusion.72
  265.1 28.9 %fusion.64 = f32[1024,1024]{1,0:T(8,128)} fusion(f32[4,19,19,1024]{3,2,1,0:T(8,128)S(1)} %subtract_multiply_fusion.1, f32[4,19,19,512]{3,2,1,0:T(8,128)S(1)} %copy-done.17, f32[4,19,19,512]{3,2,1,0:T(8,128)S(1)} %copy-done.21), kind=kOutput, calls=%fused_computation.131 | convolution fusion | flops 18171203584 | bytes 16023552 | tf_op jit(solution)/shard_map/nhwc,nhwd->cd/dot_general | solution.py:31
  294.0 4.9 copy.97
  298.9 7.0 reshape.156
  305.9 6.9 copy.95
  312.9 7.0 reshape.145
  319.9 9.4 fusion.102
  329.4 6.6 all-reduce.5
  336.0 18.9 %fusion.85 = f32[512,512]{1,0:T(8,128)} fusion(f32[4,19,19,512]{3,2,1,0:T(8,128)} %copy-done.6, f32[4,19,19,512]{3,2,1,0:T(8,128)} %get-tuple-element.152, f32[4,19,19,512]{3,2,1,0:T(8,128)} %get-tuple-element.179, f32[]{:T(128)} %get-tuple-element.142, f32[512]{0:T(512)S(1)} %get-tuple-element.129, f32[512]{0:T(512)S(1)} %get-tuple-element.130, ...), kind=kOutput, calls=%fused_computation.143 | convolution fusion | flops 4549085184 | bytes 9936532 | tf_op jit(solution)/shard_map/nhwc,nhwd->cd/dot_general | solution.py:31
  354.9 10.6 fusion.40
  365.5 5.8 all-reduce.4
  371.3 3.2 add_divide_fusion
  374.6 4.9 copy.99
  379.4 7.0 reshape.158
  386.5 3.8 fusion.38
  394.1 4.4 select_maximum_fusion
  398.5 34.3 %broadcast_select_fusion = f32[19,32,3,512]{3,1,2,0:T(8,128)S(1)} fusion(pred[32,3]{0,1:T(4,128)(4,1)S(1)} %copy-done.70, bf16[3,3,512,512]{3,2,1,0:T(8,128)(2,1)} %param.30, f32[19,4,8,5,512]{4,1,3,2,0:T(4,128)} %select_maximum_fusion), kind=kOutput, calls=%fused_computation.140 | convolution fusion | flops 49829265408 | bytes 14680160 | tf_op jit(solution)/shard_map/transpose(jvp())/conv_general_dilated | solution.py:16
  432.8 4.9 copy.103
  437.7 7.1 reshape.154
  444.8 8.4 fusion.101
  453.2 6.6 all-reduce.3
  459.9 11.3 convolution_add_fusion
  471.2 10.2 fusion.80
  481.5 108.9 %fusion.56 = f32[3,3,512,512]{3,2,1,0:T(8,128)} fusion(f32[4,19,19,512]{3,2,1,0:T(8,128)S(1)} %copy-done.9, f32[4,19,19,512]{3,2,1,0:T(8,128)S(1)} %copy-done.19), kind=kOutput, calls=%fused_computation.127 | convolution fusion | flops 38063308800 | bytes 15351808 | tf_op jit(solution)/shard_map/transpose(jvp())/conv_general_dilated | solution.py:16
  590.6 12.8 fusion.99
  603.4 5.7 all-reduce.2
  609.2 7.4 subtract_multiply_fusion
  616.6 3.0 copy-done.13
  619.5 28.9 %fusion.59 = f32[1024,1024]{1,0:T(8,128)} fusion(f32[4,19,19,1024]{3,2,1,0:T(8,128)S(1)} %subtract_multiply_fusion, f32[4,19,19,1024]{3,2,1,0:T(8,128)S(1)} %copy-done.71), kind=kOutput, calls=%fused_computation.130 | convolution fusion | flops 18169724928 | bytes 16023552 | tf_op jit(solution)/shard_map/nhwc,nhwd->cd/dot_general | solution.py:31
  648.6 341.7 %all-reduce.18.cloned.1.call-done = (f32[1024,1024]{1,0:T(8,128)}, f32[512,512]{1,0:T(8,128)}, f32[3,3,512,512]{3,2,1,0:T(8,128)}, f32[512,512]{1,0:T(8,128)}, f32[1024,1024]{1,0:T(8,128)}) async-done(((f32[1024,1024]{1,0:T(8,128)}, f32[512,512]{1,0:T(8,128)}, f32[3,3,512,512]{3,2,1,0:T(8,128)}, f32[512,512]{1,0:T(8,128)}, f32[1024,1024]{1,0:T(8,128)}), (f32[1024,1024]{1,0:T(8,128)}, f32[512,512]{1,0:T(8,128)}, ...) | async-done | bytes 19922960 | tf_op jit(solution)/shard_map/psum | solution.py:167
  990.3 10.0 copy.115
  1000.4 15.6 broadcast_multiply_fusion
  1016.0 6.9 copy.116
  1023.0 40.3 %all-reduce = (f32[1024]{0:T(1024)}, f32[1024]{0:T(1024)}, f32[512]{0:T(512)}, f32[512]{0:T(512)}, f32[512]{0:T(512)}, /*index=5*/f32[512]{0:T(512)}, f32[512]{0...) all-reduce(f32[1024]{0:T(1024)S(1)} %get-tuple-element.123, ...), channel_id=1, replica_groups=mesh['dp'=8,'bn'=4] {'dp'}, use_global_device_ids=true, to_apply=%region_44.47 | all-reduce | flops 7168 | bytes 57344 | tf_op jit(solution)/shard_map/psum | solution.py:167
  1063.2 535.9 %all-reduce.16.cloned.1.call-done = (f32[1024,1024]{1,0:T(8,128)}, f32[512,512]{1,0:T(8,128)}, f32[3,3,512,512]{3,2,1,0:T(8,128)}, f32[512,512]{1,0:T(8,128)}, f32[1024,1024]{1,0:T(8,128)}) async-done(((f32[1024,1024]{1,0:T(8,128)}, f32[512,512]{1,0:T(8,128)}, f32[3,3,512,512]{3,2,1,0:T(8,128)}, f32[512,512]{1,0:T(8,128)}, f32[1024,1024]{1,0:T(8,128)}), (f32[1024,1024]{1,0:T(8,128)}, f32[512,512]{1,0:T(8,128)}, ...) | async-done | bytes 19922960 | tf_op jit(solution)/shard_map/psum | solution.py:167
  1599.2 5.1 copy.238
  1606.9 4.8 copy.240
  (166 shorter events, 18.9 us)
Async XLA Ops:
  7.2 983.1 %all-reduce.18.cloned.1.call-start = ((), (), s32[]{:S(2)}) async-start(), calls=%async_computation.1 | async-start | bytes 39845888 | tf_op jit(solution)/shard_map/psum | solution.py:167
  9.0 462.2 %copy-start.10 = (f32[4,19,19]{2,1,0:T(8,128)}, f32[4,19,19]{2,1,0:T(8,128)S(1)}, u32[]{:S(2)}) copy-start(f32[4,19,19]{2,1,0:T(8,128)S(1)} %and_convert_fusion) | copy-start | bytes 17332
  9.7 29.9 %copy-start.32 = (f32[1024]{0:T(1024)S(1)}, f32[1024]{0:T(1024)}, u32[]{:S(2)}) copy-start(f32[1024]{0:T(1024)} %param.25) | copy-start | bytes 12292
  9.7 29.9 %copy-start.42 = (f32[1024]{0:T(1024)S(1)}, f32[1024]{0:T(1024)}, u32[]{:S(2)}) copy-start(f32[1024]{0:T(1024)} %param.26) | copy-start | bytes 12292
  39.6 7.9 copy-start.28
  39.6 7.9 copy-start.30
  39.6 7.8 copy-start.68
  47.5 5.4 copy-start.5
  47.5 12.0 copy-start.38
  47.5 12.0 copy-start.40
  59.5 4.9 copy-start.34
  59.5 4.9 copy-start.36
  145.4 10.2 copy-start.51
  145.4 10.2 copy-start.57
  175.3 6.9 copy-start.27
  182.3 5.3 copy-start.6
  182.3 12.0 copy-start.49
  182.3 12.0 copy-start.50
  198.9 14.4 copy-start.20
  198.9 21.8 %copy-start.44 = (f32[1024]{0:T(1024)S(1)}, f32[1024]{0:T(1024)}, u32[]{:S(2)}) copy-start(f32[1024]{0:T(1024)} %param.37) | copy-start | bytes 12292
  198.9 21.8 %copy-start.56 = (f32[1024]{0:T(1024)S(1)}, f32[1024]{0:T(1024)}, u32[]{:S(2)}) copy-start(f32[1024]{0:T(1024)} %param.38) | copy-start | bytes 12292
  243.7 7.4 copy-start.45
  243.8 7.4 copy-start.47
  243.8 7.4 copy-start.67
  251.1 13.9 copy-start.17
  251.2 13.9 copy-start.21
  265.1 28.9 %copy-start.3 = (f32[19,32,3,512]{3,1,2,0:T(8,128)S(1)}, f32[19,32,3,512]{3,1,2,0:T(8,128)}, u32[]{:S(2)}) copy-start(f32[19,32,3,512]{3,1,2,0:T(8,128)} %get-tuple-element.156) | copy-start | bytes 11206660
  335.9 18.9 %copy-start.58 = (f32[512]{0:T(512)}, f32[512]{0:T(512)S(1)}, u32[]{:S(2)}) copy-start(f32[512]{0:T(512)S(1)} %get-tuple-element.129) | copy-start | bytes 6148
  335.9 18.9 %copy-start.60 = (f32[512]{0:T(512)}, f32[512]{0:T(512)S(1)}, u32[]{:S(2)}) copy-start(f32[512]{0:T(512)S(1)} %get-tuple-element.130) | copy-start | bytes 6148
  335.9 18.9 %copy-start.4 = (f32[4,19,19,512]{3,2,1,0:T(8,128)S(1)}, f32[4,19,19,512]{3,2,1,0:T(8,128)}, u32[]{:S(2)}) copy-start(f32[4,19,19,512]{3,2,1,0:T(8,128)} %get-tuple-element.179) | copy-start | bytes 8871940
  335.9 18.9 %copy-start.23 = (f32[19,4,24,512]{3,2,1,0:T(8,128)S(1)}, f32[19,4,24,512]{3,2,1,0:T(8,128)}, u32[]{:S(2)}) copy-start(f32[19,4,24,512]{3,2,1,0:T(8,128)} %reshape.156) | copy-start | bytes 11206660
  335.9 18.9 %copy-start.24 = (f32[19,4,24,512]{3,2,1,0:T(8,128)S(1)}, f32[19,4,24,512]{3,2,1,0:T(8,128)}, u32[]{:S(2)}) copy-start(f32[19,4,24,512]{3,2,1,0:T(8,128)} %reshape.145) | copy-start | bytes 11206660
  335.9 18.9 %copy-start.25 = (f32[4,19,19,512]{3,2,1,0:T(8,128)S(1)}, f32[4,19,19,512]{3,2,1,0:T(8,128)}, u32[]{:S(2)}) copy-start(f32[4,19,19,512]{3,2,1,0:T(8,128)} %get-tuple-element.152) | copy-start | bytes 8871940
  437.7 7.1 copy-start.35
  437.7 7.1 copy-start.37
  437.7 7.1 copy-start.39
  437.7 7.1 copy-start.41
  444.8 15.0 copy-start.69
  459.8 11.4 copy-start.62
  459.8 11.4 copy-start.64
  459.8 11.4 copy-start.2
  459.8 11.3 copy-start.15
  459.9 11.3 copy-start.22
  471.2 10.3 copy-start.9
  471.2 10.2 copy-start.19
  481.5 109.0 %copy-start.7 = (f32[4,19,19,512]{3,2,1,0:T(8,128)S(1)}, f32[4,19,19,512]{3,2,1,0:T(8,128)}, u32[]{:S(2)}) copy-start(f32[4,19,19,512]{3,2,1,0:T(8,128)} %get-tuple-element.161) | copy-start | bytes 8871940
  481.5 109.0 %copy-start.11 = (f32[4,19,19]{2,1,0:T(8,128)S(1)}, f32[4,19,19]{2,1,0:T(8,128)}, u32[]{:S(2)}) copy-start(f32[4,19,19]{2,1,0:T(8,128)} %copy-done.10) | copy-start | bytes 17332
  481.5 109.0 %copy-start.18 = (f32[4,19,19,512]{3,2,1,0:T(8,128)S(1)}, f32[4,19,19,512]{3,2,1,0:T(8,128)}, u32[]{:S(2)}) copy-start(f32[4,19,19,512]{3,2,1,0:T(8,128)} %convolution_add_fusion) | copy-start | bytes 8871940
  481.5 109.0 %copy-start.29 = (f32[1024]{0:T(1024)S(1)}, f32[1024]{0:T(1024)}, u32[]{:S(2)}) copy-start(f32[1024]{0:T(1024)} %copy-done.28) | copy-start | bytes 12292
  481.5 109.0 %copy-start.31 = (f32[1024]{0:T(1024)S(1)}, f32[1024]{0:T(1024)}, u32[]{:S(2)}) copy-start(f32[1024]{0:T(1024)} %copy-done.30) | copy-start | bytes 12292
  481.5 109.0 %copy-start.33 = (f32[1024]{0:T(1024)S(1)}, f32[1024]{0:T(1024)}, u32[]{:S(2)}) copy-start(f32[1024]{0:T(1024)} %param.25) | copy-start | bytes 12292
  481.5 109.0 %copy-start.43 = (f32[1024]{0:T(1024)S(1)}, f32[1024]{0:T(1024)}, u32[]{:S(2)}) copy-start(f32[1024]{0:T(1024)} %param.26) | copy-start | bytes 12292
  609.1 10.4 copy-start.71
  648.5 950.6 %all-reduce.16.cloned.1.call-start = ((), (), s32[]{:S(2)}) async-start(), calls=%async_computation | async-start | bytes 39845888 | tf_op jit(solution)/shard_map/psum | solution.py:167
  1015.9 7.0 copy-start.46
  1015.9 7.0 copy-start.48
  1016.0 7.0 copy-start.53
  1016.0 7.0 copy-start.55
  1016.0 7.0 copy-start.59
  1016.0 7.0 copy-start.61
  1016.0 7.0 copy-start.63
  1016.0 7.0 copy-start.65
  1599.2 7.7 copy-start.12
  1606.9 6.3 copy-start.14
  (10 other events, 38.1 us)
Sparse Core Ops, SparseCore 0:
  648.6 341.6 all-reduce.17
  995.5 603.6 all-reduce.15
